TPU v7x, 512 devices: a whole 4x8x8 slice. The times are simulated.
512 devices in a mesh: row: 16 (over y, core), col: 32 (over z, x).
Axes of the slice: x: 4, y: 8, z: 8, core: 2. Of those that a mesh axis runs over, the one named last changes fastest.
Arguments:
- stored_inverse: bfloat16 [6, 16, 3, 32, 256, 256], P(None, 'row', None, 'col'), may hold values from -6 to 6
- panel_first: bfloat16 [6, 16, 256, 256], P(None, 'row', 'col'), may hold values from -0.046875 to 0.046875
- panel_second: bfloat16 [6, 16, 256, 256], P(None, 'row', 'col'), may hold values from -0.0546875 to 0.0546875
- panel_link: bfloat16 [256, 256], replicated, may hold values from -0.375 to 0.375
- inv_first: float32 [256, 256], replicated, as said below
- inv_second: float32 [256, 256], replicated, as said below
- struct_first: int32 [72], replicated, may hold values from 0 to 95, as said below
- struct_second: int32 [48], replicated, may hold values from 0 to 95, as said below
Outputs:
- column_first: float32 [6, 16, 256, 256], P(None, 'row', 'col')
- column_second: float32 [6, 16, 256, 256], P(None, 'row', 'col')
- diag_first: float32 [256, 256], P('col')
- link_block: float32 [256, 256], P('col')
- diag_second: float32 [256, 256], P('col')
Inputs may be any that keep to these rules, and one draw needn't show every extreme that they name: `struct_first`: 72 distinct block indices in increasing order; the last is always 96 - 1. `struct_second`: 48 distinct block indices in increasing order, each also listed in struct_first; the last is always 96 - 1; the second supernode's whole structure is the first supernode together with these blocks. `inv_first`: lower triangular with a positive diagonal. `inv_second`: lower triangular with a positive diagonal.
All inputs are finite; a program needn't handle non-finite values.
Results may differ from a plain program's by a relative error of at most 0.0041.
Values may be sent and summed in bfloat16 or wider, within the bound.
A program may use at most 64 MiB of HBM per device.

v0:
```python
import jax
import jax.numpy as jnp
from jax import lax
from jax.sharding import PartitionSpec as P

precise = lax.Precision.HIGHEST


def spread(value, axis, root):
    mine = lax.axis_index(axis) == root
    return lax.psum(jnp.where(mine, value, jnp.zeros_like(value)), axis)


def listed_rows(row_ids, struct):
    return jnp.any(row_ids[:, None] == struct[None, :], axis=1)


def factor_slice(panel_rows, inverse, keep_rows):
    product = jnp.einsum("kij,jl->kil", panel_rows.astype(jnp.float32), inverse, precision=precise)
    return jnp.where(keep_rows[:, None, None], product, 0.0).astype(jnp.bfloat16)


def spread_factor(factor_part, cycle_ratio, pick_index, root_row):
    gathered = lax.all_gather(factor_part, "col", axis=1, tiled=True)
    height = gathered.shape[-2]
    breadth = gathered.shape[-1]
    arrived = spread(gathered, "row", root_row)
    grouped = arrived.reshape(-1, cycle_ratio, height, breadth)
    result = lax.dynamic_index_in_dim(grouped, pick_index, 1, keepdims=False)
    return result


def column_sums(stored, factors):
    summed = lax.psum_scatter(
        jnp.einsum("abij,bjl->ial", stored, factors, preferred_element_type=jnp.float32),
        "col",
        scatter_dimension=0,
        tiled=True,
    )
    return jnp.transpose(summed, (1, 0, 2))


def body(
    stored_inverse,
    panel_first,
    panel_second,
    panel_link,
    inv_first,
    inv_second,
    struct_first,
    struct_second,
):
    n_row = lax.axis_size("row")
    n_col = lax.axis_size("col")
    here_row = lax.axis_index("row")
    here_col = lax.axis_index("col")
    row_blocks = stored_inverse.shape[0]
    col_blocks = stored_inverse.shape[2]
    block_width = stored_inverse.shape[-1]
    slab_rows = block_width // n_col
    cycle_ratio = n_col // n_row
    stored = stored_inverse.reshape(row_blocks, col_blocks, block_width, block_width)
    row_ids = jnp.arange(row_blocks, dtype=jnp.int32) * n_row + here_row
    keep_first = listed_rows(row_ids, struct_first)
    keep_second = listed_rows(row_ids, struct_second)
    pick_index = here_col // n_row
    root_row = here_col % n_row
    part_first = factor_slice(
        panel_first.reshape(row_blocks, slab_rows, block_width), inv_first, keep_first
    )
    part_second = factor_slice(
        panel_second.reshape(row_blocks, slab_rows, block_width), inv_second, keep_second
    )
    link_wide = jnp.dot(panel_link.astype(jnp.float32), inv_second, precision=precise)
    factors_first = spread_factor(part_first, cycle_ratio, pick_index, root_row)
    sums_first = column_sums(stored, factors_first)
    factors_second = spread_factor(part_second, cycle_ratio, pick_index, root_row)
    sums_second = column_sums(stored, factors_second)
    column_first = jnp.where(keep_first[:, None, None], -sums_first, 0.0)
    first_term = jnp.einsum(
        "kij,kil->jl", part_first.astype(jnp.float32), column_first, precision=precise
    )
    top_term = jnp.einsum(
        "kij,kil->jl", column_first, part_second.astype(jnp.float32), precision=precise
    )
    carried = jnp.einsum("kij,jl->kil", column_first, link_wide, precision=precise)
    column_second = jnp.where(keep_second[:, None, None], -(sums_second + carried), 0.0)
    second_term = jnp.einsum(
        "kij,kil->jl", part_second.astype(jnp.float32), column_second, precision=precise
    )
    offset = here_col * slab_rows
    gram_first = jnp.dot(inv_first.T, inv_first, precision=precise)
    gram_second = jnp.dot(inv_second.T, inv_second, precision=precise)
    total_first, total_top, total_second = lax.psum(
        (first_term, top_term, second_term), ("row", "col")
    )
    diag_whole = gram_first - total_first
    link_whole = -(total_top + jnp.dot(diag_whole, link_wide, precision=precise))
    second_whole = gram_second - total_second - jnp.dot(link_wide.T, link_whole, precision=precise)
    diag_first = lax.dynamic_slice_in_dim(diag_whole, offset, slab_rows, 0)
    link_block = lax.dynamic_slice_in_dim(link_whole, offset, slab_rows, 0)
    diag_second = lax.dynamic_slice_in_dim(second_whole, offset, slab_rows, 0)
    return (
        column_first.reshape(row_blocks, 1, slab_rows, block_width),
        column_second.reshape(row_blocks, 1, slab_rows, block_width),
        diag_first,
        link_block,
        diag_second,
    )


def solution(mesh):
    placed = (
        P(None, "row", None, "col", None, None),
        P(None, "row", "col", None),
        P(None, "row", "col", None),
        P(),
        P(),
        P(),
        P(),
        P(),
    )
    return jax.shard_map(
        body,
        mesh=mesh,
        in_specs=placed,
        out_specs=(
            P(None, "row", "col", None),
            P(None, "row", "col", None),
            P("col", None),
            P("col", None),
            P("col", None),
        ),
        check_vma=False,
    )
```

profile of v0, /device:TPU:1, one launch (start us, length us, event | category | flops | bytes accessed | tf_op | source)
XLA Modules:
  0.0 963.5 jit_solution(13383805086381771064)
XLA Ops:
  7.2 0.0 copy-start
  7.2 0.0 all-reduce.7.cloned.1.call-start
  7.3 1.0 compare_reduce_fusion
  8.3 1.2 fusion.14
  9.5 43.0 %all_gather.7 = bf16[6,256,256]{2,1,0:T(8,128)(2,1)S(1)} all-gather(bf16[6,8,256]{2,1,0:T(8,128)(2,1)S(1)} %fusion.14), channel_id=1, replica_groups=mesh['row'=16,'col'=32] {'col'}, dimensions={1}, use_global_device_ids=true | all-gather | bytes 811008 | tf_op jit(solution)/shard_map/all_gather | solution.py:24
  52.4 0.8 compare_reduce_fusion.1
  53.3 1.2 fusion.13
  54.5 34.8 %all_gather.6 = bf16[6,256,256]{2,1,0:T(8,128)(2,1)S(1)} all-gather(bf16[6,8,256]{2,1,0:T(8,128)(2,1)S(1)} %fusion.13), channel_id=1, replica_groups=mesh['row'=16,'col'=32] {'col'}, dimensions={1}, use_global_device_ids=true | all-gather | bytes 811008 | tf_op jit(solution)/shard_map/all_gather | solution.py:24
  89.3 1.0 broadcast_select_fusion
  90.2 0.9 broadcast_select_fusion.1
  91.2 0.0 all-reduce.7.cloned.1.call-update
  91.2 0.0 reduce-scatter.3.cloned.1.call-start
  91.3 131.8 %all-reduce.7.cloned.1.call-done = (bf16[3,2,256,256]{3,2,1,0:T(8,128)(2,1)}, bf16[3,2,256,256]{3,2,1,0:T(8,128)(2,1)}) async-done(((bf16[3,2,256,256]{3,2,1,0:T(8,128)(2,1)}, bf16[3,2,256,256]{3,2,1,0:T(8,128)(2,1)}), (bf16[3,2,256,256]{3,2,1,0:T(8,128)(2,1)}, bf16[3,2,256,256]{3,2,1,0:T(8,128)(2,1)})) %all-reduce.7.cloned.1.call-update) | async-done | bytes 1572880 | tf_op jit(solution)/shard_map/psum | solution.py:11
  223.1 0.0 copy-done
  223.1 3.0 fusion.4
  226.0 3.0 copy.31
  229.0 0.0 reduce-scatter.3.cloned.1.call-update
  229.0 0.0 reduce-scatter.5.cloned.1.call-start
  229.1 0.0 copy-start.1
  229.1 0.0 copy-start.3
  229.1 3.0 fusion.7
  232.1 0.0 reduce-scatter.5.cloned.1.call-update
  232.1 0.0 all-reduce.5.cloned.1.call-start
  232.2 0.0 copy-done.1
  232.2 0.0 copy-done.3
  232.2 0.3 fusion.31
  232.5 0.0 copy-start.2
  232.5 214.8 %reduce-scatter.3.cloned.1.call-done = f32[8,6,256]{2,1,0:T(8,128)} async-done(((f32[256,6,256]{2,1,0:T(8,128)}), f32[8,6,256]{2,1,0:T(8,128)}) %reduce-scatter.3.cloned.1.call-update) | async-done | bytes 49168 | tf_op jit(solution)/shard_map/reduce_scatter | solution.py:34
  447.3 0.9 fusion.23
  448.2 1.0 convolution_bitcast_fusion.2
  449.2 1.0 convolution_bitcast_fusion.1
  450.3 220.6 %reduce-scatter.5.cloned.1.call-done = f32[8,6,256]{2,0,1:T(8,128)} async-done(((f32[256,6,256]{2,0,1:T(8,128)}), f32[8,6,256]{2,0,1:T(8,128)}) %reduce-scatter.5.cloned.1.call-update) | async-done | bytes 49168 | tf_op jit(solution)/shard_map/reduce_scatter | solution.py:34
  670.9 1.0 fusion.12
  671.9 0.0 copy-start.4
  671.9 0.6 copy-done.4
  672.5 1.0 convolution_bitcast_fusion
  673.5 0.0 all-reduce.5.cloned.1.call-update
  673.6 0.6 fusion.32
  674.2 0.6 copy.37
  674.8 276.7 %all-reduce.5.cloned.1.call-done = (f32[256,256]{1,0:T(8,128)}, f32[256,256]{1,0:T(8,128)}, f32[256,256]{1,0:T(8,128)}) async-done(((f32[256,256]{1,0:T(8,128)}, f32[256,256]{1,0:T(8,128)}, f32[256,256]{1,0:T(8,128)}), (f32[256,256]{1,0:T(8,128)}, f32[256,256]{1,0:T(8,128)}, f32[256,256]{1,0:T(8,128)})) %all-reduce.5.cloned.1.call-update) | async-done | bytes 786448 | tf_op jit(solution)/shard_map/psum | solution.py:94
  951.5 0.0 copy-done.2
  951.5 1.5 convolution_subtract_fusion
  953.1 1.3 fusion.10
  954.4 0.6 fusion.33
  955.0 0.6 constant_dynamic-slice_fusion.1
  955.6 1.3 dynamic-slice_subtract_fusion
  (1 shorter events, 0.0 us)
Async XLA Ops:
  7.2 215.9 %copy-start = (bf16[6,1,3,1,256,256]{5,4,3,2,1,0:T(8,128)(2,1)S(1)}, bf16[6,1,3,1,256,256]{5,4,3,2,1,0:T(8,128)(2,1)}, u32[]{:S(2)}) copy-start(bf16[6,1,3,1,256,256]{5,4,3,2,1,0:T(8,128)(2,1)} %param.8) | copy-start | bytes 7077892
  7.2 215.9 %all-reduce.7.cloned.1.call-start = ((), (), s32[]{:S(2)}) async-start(), calls=%async_computation.5 | async-start | bytes 3145728 | tf_op jit(solution)/shard_map/psum | solution.py:11
  91.2 356.1 %reduce-scatter.3.cloned.1.call-start = ((), (), s32[]{:S(2)}) async-start(), calls=%async_computation.2 | async-start | bytes 2162688 | tf_op jit(solution)/shard_map/reduce_scatter | solution.py:34
  229.0 441.8 %reduce-scatter.5.cloned.1.call-start = ((), (), s32[]{:S(2)}) async-start(), calls=%async_computation.3 | async-start | bytes 1622016 | tf_op jit(solution)/shard_map/reduce_scatter | solution.py:34
  229.1 3.1 copy-start.1
  229.1 3.1 copy-start.3
  232.1 719.4 %all-reduce.5.cloned.1.call-start = ((), (), s32[]{:S(2)}) async-start(), calls=%async_computation.4 | async-start | bytes 1572864 | tf_op jit(solution)/shard_map/psum | solution.py:94
  232.5 719.0 %copy-start.2 = (f32[256,256]{1,0:T(8,128)S(1)}, f32[256,256]{1,0:T(8,128)}, u32[]{:S(2)}) copy-start(f32[256,256]{1,0:T(8,128)} %param.12) | copy-start | bytes 786436
  671.9 0.6 copy-start.4
Sparse Core Ops, SparseCore 0:
  91.3 131.7 all-reduce.6
  229.2 218.1 reduce-scatter.2
  451.7 219.0 reduce-scatter.4
  676.2 275.2 all-reduce.4
where the time goes:
time: 964 us; the launch traced here: 963 us
  waiting for transfers between devices  844 us (88%)
  blocking collectives  77.8 us (8%)
  matrix products  16.8 us (2%)
  between operations  13.9 us (1%)
    reduce_scatter x2, waiting for transfers between devices, column_sums(): lax.psum_scatter(jnp.einsum('abij,bjl->ial', stored, factors, preferred_e...  435 us
    psum x1, waiting for transfers between devices, body(): lax.psum((first_term, top_term, second_term), ('row', 'col'))  277 us
    psum x1, waiting for transfers between devices, spread(): return lax.psum(jnp.where(mine, value, jnp.zeros_like(value)), axis)  132 us
    all_gather x2, blocking collectives, spread_factor(): gathered = lax.all_gather(factor_part, 'col', axis=1, tiled=True)  77.8 us
  transfers between devices with their start and end apart: 4, of which 4 were waited for; matrix products, arithmetic and copies ran while one was open for 1% of the time, Pallas kernels for 0%

commit v1 on v0

v1 whole, which is shorter than its diff:
```python
import jax
import jax.numpy as jnp
from jax import lax
from jax.experimental import pallas as pl
from jax.experimental.pallas import tpu as pltpu
from jax.sharding import PartitionSpec as P

NX, NY, NZ = 4, 8, 8
F32, BF16 = jnp.float32, jnp.bfloat16
precise = lax.Precision.HIGHEST


def dev(row, col):
    return {"row": row, "col": col}


def fdot(a, b):
    return jnp.dot(a, b, preferred_element_type=F32, precision=precise)


def tdot(a, b):
    return lax.dot_general(a, b, (((0,), (0,)), ((), ())), preferred_element_type=F32, precision=precise)


def wait_bytes(ref, sem):
    pltpu.make_async_copy(ref, ref, sem).wait()


def listed(struct_ref, block):
    hit = jnp.where(struct_ref[...] == block, 1.0, 0.0)
    return jnp.max(hit, axis=1, keepdims=True)


def kernel(
    s_hbm, p1_hbm, p2_hbm, link_hbm, inv1_hbm, inv2_hbm, st1, st2,
    col1, col2, diag1, link, diag2,
    s_v, p_v, link_v, inv_v, wide, gram1, gram2, raw, fac, own_fac,
    half_out, half_in, pair_out, pair_in, kept, z_out, z_in,
    ea_out, ea_in, ea_z, ea_zin, ea_y, ea_yin,
    eb_out, eb_in, eb_z, eb_zin, eb_y, eb_yin, rest, carry,
    load_sem, a_send, send_sem, recv_sem,
):
    row, col = lax.axis_index("row"), lax.axis_index("col")
    y, core = lax.div(row, 2), lax.rem(row, 2)
    z, x = lax.div(col, NX), lax.rem(col, NX)
    quad = lax.rem(y, 4)
    panels = (p1_hbm, p2_hbm)

    loads = [
        pltpu.make_async_copy(p1_hbm, p_v.at[0], load_sem.at[0]),
        pltpu.make_async_copy(p2_hbm, p_v.at[1], load_sem.at[1]),
        pltpu.make_async_copy(inv1_hbm, inv_v.at[0], load_sem.at[2]),
        pltpu.make_async_copy(inv2_hbm, inv_v.at[1], load_sem.at[3]),
        pltpu.make_async_copy(link_hbm, link_v, load_sem.at[4]),
        pltpu.make_async_copy(s_hbm, s_v, load_sem.at[5]),
    ]
    for load in loads:
        load.start()

    barrier = pltpu.get_barrier_semaphore()

    def greet(r, c):
        pl.semaphore_signal(barrier, inc=1, device_id=dev(r, c), device_id_type=pl.DeviceIdType.MESH)

    src_row = lax.rem(col, 16)
    for slot in range(4):
        src_col = 4 * (2 * quad + core) + slot
        me = jnp.logical_and(src_row == row, src_col == col)

        @pl.when(jnp.logical_not(me))
        def _():
            greet(src_row, src_col)

    for d in range(1, NX):
        greet(row, 4 * z + lax.rem(x + d, NX))
    for d in range(1, NZ):
        greet(row, 4 * lax.rem(z + d, NZ) + x)
    for d in range(0, NY):
        for k in range(0, 2):
            if d or k:
                greet(2 * lax.rem(y + d, NY) + lax.rem(core + k, 2), col)

    targets = []
    others = 3 + 7 + 15
    for zhi in range(2):
        for k in range(2):
            r_t = 2 * (lax.div(z, 2) + 4 * k) + lax.rem(z, 2)
            c_t = row + 16 * zhi
            me = jnp.logical_and(r_t == row, c_t == col)
            others = others + jnp.where(me, 0, 1)
            targets.append((zhi, k, r_t, c_t, me))
    pl.semaphore_wait(barrier, others)

    def stage_a(sn, zhi, k, r_t, c_t):
        spot = raw.at[sn, :, lax.div(col, 8), lax.rem(lax.div(col, 4), 2), lax.rem(col, 4)]
        return (
            pltpu.make_async_remote_copy(
                panels[sn].at[:, zhi], spot, a_send.at[sn, 2 * zhi + k], recv_sem.at[0, sn],
                device_id=dev(r_t, c_t), device_id_type=pl.DeviceIdType.MESH),
            pltpu.make_async_copy(panels[sn].at[:, zhi], spot, recv_sem.at[0, sn]),
        )

    for sn in range(2):
        for zhi, k, r_t, c_t, me in targets:
            far, near = stage_a(sn, zhi, k, r_t, c_t)

            @pl.when(jnp.logical_not(me))
            def _():
                far.start()

            @pl.when(me)
            def _():
                near.start()

    for load in loads[:5]:
        load.wait()
    for sn in range(2):
        product = fdot(p_v[sn].astype(F32).reshape(48, 256), inv_v[sn])
        own_fac[sn] = product
    for block in range(6):
        number = block * 16 + row
        m1, m2 = listed(st1, number), listed(st2, number)
        own_fac[0, 8 * block:8 * block + 8, :] = (own_fac[0, 8 * block:8 * block + 8, :] * m1).astype(BF16).astype(F32)
        own_fac[1, 8 * block:8 * block + 8, :] = (own_fac[1, 8 * block:8 * block + 8, :] * m2).astype(BF16).astype(F32)
    wide[...] = fdot(link_v[...].astype(F32), inv_v[1])
    gram1[...] = tdot(inv_v[0], inv_v[0])

    def remote(src, dst, stage, sn, r, c):
        copy = pltpu.make_async_remote_copy(
            src, dst, send_sem.at[stage, sn], recv_sem.at[stage, sn],
            device_id=dev(r, c), device_id_type=pl.DeviceIdType.MESH)
        copy.start()

    for sn in range(2):
        wait_bytes(raw.at[sn, :, quad, core], recv_sem.at[0, sn])
        spot = raw.at[sn, :, quad, core]
        for d in (2, 1, 7):
            remote(spot, spot, 1, sn, 2 * lax.rem(y + d, NY) + core, col)
    gram2[...] = tdot(inv_v[1], inv_v[1]) + tdot(wide[...], fdot(gram1[...], wide[...]))
    for sn in range(2):
        wait_bytes(raw.at[sn, :, pl.ds(0, 3), core], recv_sem.at[1, sn])
        spot = raw.at[sn, :, :, core]
        remote(spot, spot, 2, sn, 2 * y + 1 - core, col)
    loads[5].wait()

    x1 = x + 1 - 2 * lax.rem(x, 2)
    x3 = 3 - x
    rel = (x, x1, lax.rem(x + 2, 4), x3)
    first_peer = (x1, x3)
    second_peer = (x3, x1)
    structs = (st1, st2)

    for sn in range(2):
        wait_bytes(raw.at[sn, :, :, core], recv_sem.at[2, sn])
        upper = inv_v[sn].astype(BF16)
        lower = (inv_v[sn] - upper.astype(F32)).astype(BF16)
        for b in range(3):
            rows = raw[sn, b].astype(F32).reshape(256, 256).astype(BF16)
            product = jnp.dot(rows, upper, preferred_element_type=F32) + jnp.dot(rows, lower, preferred_element_type=F32)
            fac[sn, b] = (product * listed(structs[sn], b * 32 + col)).astype(BF16)
        for half in range(2):
            def block_row(step, _):
                a = 3 * half + step
                total = jnp.dot(s_v[a, 0], fac[sn, 0], preferred_element_type=F32)
                total += jnp.dot(s_v[a, 1], fac[sn, 1], preferred_element_type=F32)
                total += jnp.dot(s_v[a, 2], fac[sn, 2], preferred_element_type=F32)
                for xd in range(NX):
                    slot = lax.rem(rel[xd] + 3, 4) if half == 0 else 3 - rel[xd]
                    for zd in range(NZ):
                        at = 8 * (4 * zd + xd)
                        half_out[sn, half, slot, zd, step] = total[at:at + 8, :].astype(BF16)
                return 0

            lax.fori_loop(0, 3, block_row, 0)
            remote(half_out.at[sn, half, pl.ds(0, 2)], half_in.at[sn, half], 3 + half, sn, row, 4 * z + first_peer[half])

    for sn in range(2):
        for half in range(2):
            wait_bytes(half_in.at[sn, half], recv_sem.at[3 + half, sn])
            pair_out[sn, half] = (half_out[sn, half, 2].astype(F32) + half_in[sn, half, 1].astype(F32)).astype(BF16)
            remote(pair_out.at[sn, half], pair_in.at[sn, half], 5 + half, sn, row, 4 * z + second_peer[half])
            kept[half] = half_out[sn, half, 3].astype(F32) + half_in[sn, half, 0].astype(F32)
        for half in range(2):
            wait_bytes(pair_in.at[sn, half], recv_sem.at[5 + half, sn])
            z_out[sn, :, 3 * half:3 * half + 3] = (kept[half] + pair_in[sn, half].astype(F32)).astype(BF16)
        for d in (4, 3, 5, 2, 6, 1, 7):
            to = lax.rem(z + d, NZ)
            remote(z_out.at[sn, to], z_in.at[sn, d - 1], 7, sn, row, 4 * to + x)

    def z_total(sn):
        wait_bytes(z_in.at[sn], recv_sem.at[7, sn])
        total = z_out[sn, z].astype(F32)
        for d in range(7):
            total += z_in[sn, d].astype(F32)
        return total

    total = z_total(0)
    for block in range(6):
        col1[block] = total[block] * (-listed(st1, block * 16 + row))
    first = tdot(own_fac[0], col1[...].reshape(48, 256))
    top = tdot(col1[...].reshape(48, 256), own_fac[1])

    def spread_rows(out, m, matrix):
        for xd in range(NX):
            for zd in range(NZ):
                at = 8 * (4 * zd + xd)
                out[xd, zd, m] = matrix[at:at + 8, :].astype(BF16)

    spread_rows(ea_out, 0, first)
    spread_rows(ea_out, 1, top)
    for d in (2, 1, 3):
        to = lax.rem(x + d, NX)
        remote(ea_out.at[to], ea_in.at[d - 1], 8, 0, row, 4 * z + to)
    rest[...] = tdot(wide[...], fdot(first, wide[...]) - top)
    carry[...] = fdot(col1[...].reshape(48, 256), wide[...])

    total = z_total(1).reshape(48, 256) + carry[...]
    for block in range(6):
        col2[block] = total[8 * block:8 * block + 8, :] * (-listed(st2, block * 16 + row))
    second = tdot(own_fac[1], col2[...].reshape(48, 256)) + rest[...]
    spread_rows(eb_out, 0, second)
    for d in (2, 1, 3):
        to = lax.rem(x + d, NX)
        remote(eb_out.at[to], eb_in.at[d - 1], 8, 1, row, 4 * z + to)

    groups = ((ea_out, ea_in, ea_z, ea_zin, ea_y, ea_yin), (eb_out, eb_in, eb_z, eb_zin, eb_y, eb_yin))
    for g, (g_out, g_in, g_z, g_zin, g_y, g_yin) in enumerate(groups):
        wait_bytes(g_in, recv_sem.at[8, g])
        total = g_out[x].astype(F32)
        for d in range(3):
            total += g_in[d].astype(F32)
        g_z[...] = total.astype(BF16)
        for d in (4, 3, 5, 2, 6, 1, 7):
            to = lax.rem(z + d, NZ)
            remote(g_z.at[to], g_zin.at[d - 1], 9, g, row, 4 * to + x)
    for g, (g_out, g_in, g_z, g_zin, g_y, g_yin) in enumerate(groups):
        wait_bytes(g_zin, recv_sem.at[9, g])
        total = g_z[z].astype(F32)
        for d in range(7):
            total += g_zin[d].astype(F32)
        g_y[...] = total
        for d in (4, 3, 5, 2, 6, 1, 7, 0):
            for k in range(2):
                if d or k:
                    to = 2 * lax.rem(y + d, NY) + lax.rem(core + k, 2)
                    remote(g_y, g_yin.at[2 * d + k - 1], 10, g, to, col)

    def y_total(g):
        g_y, g_yin = groups[g][4:]
        wait_bytes(g_yin, recv_sem.at[10, g])
        total = g_y[...]
        for d in range(15):
            total += g_yin[d]
        return total

    at = pl.multiple_of(8 * col, 8)
    total = y_total(0)
    diag1[...] = gram1[pl.ds(at, 8), :] - total[0]
    link[...] = -(total[1] + fdot(diag1[...], wide[...]))
    diag2[...] = gram2[pl.ds(at, 8), :] - y_total(1)[0]

    for sn in range(2):
        for zhi, k, r_t, c_t, me in targets:
            far, _ = stage_a(sn, zhi, k, r_t, c_t)

            @pl.when(jnp.logical_not(me))
            def _():
                far.wait_send()

        wait_bytes(raw.at[sn, :, pl.ds(0, 3), core], send_sem.at[1, sn])
        wait_bytes(raw.at[sn, :, :, core], send_sem.at[2, sn])
        for half in range(2):
            wait_bytes(half_in.at[sn, half], send_sem.at[3 + half, sn])
            wait_bytes(pair_in.at[sn, half], send_sem.at[5 + half, sn])
        wait_bytes(z_in.at[sn], send_sem.at[7, sn])
        wait_bytes(groups[sn][1], send_sem.at[8, sn])
        wait_bytes(groups[sn][3], send_sem.at[9, sn])
        wait_bytes(groups[sn][5], send_sem.at[10, sn])


def body(stored_inverse, panel_first, panel_second, panel_link, inv_first, inv_second, struct_first, struct_second):
    anywhere = pl.BlockSpec(memory_space=pl.ANY)
    vmem = pl.BlockSpec(memory_space=pltpu.VMEM)

    def e_scratch(n):
        return [
            pltpu.VMEM((4, 8, n, 8, 256), BF16), pltpu.VMEM((3, 8, n, 8, 256), BF16),
            pltpu.VMEM((8, n, 8, 256), BF16), pltpu.VMEM((7, n, 8, 256), BF16),
            pltpu.VMEM((n, 8, 256), F32), pltpu.VMEM((15, n, 8, 256), F32),
        ]

    c1, c2, d1, lk, d2 = pl.pallas_call(
        kernel,
        out_shape=[jax.ShapeDtypeStruct((6, 8, 256), F32)] * 2 + [jax.ShapeDtypeStruct((8, 256), F32)] * 3,
        in_specs=[anywhere] * 6 + [vmem] * 2,
        out_specs=[vmem] * 5,
        scratch_shapes=[
            pltpu.VMEM((6, 3, 256, 256), BF16),
            pltpu.VMEM((2, 3, 2, 8, 256), BF16),
            pltpu.VMEM((256, 256), BF16),
            pltpu.VMEM((2, 256, 256), F32),
            pltpu.VMEM((256, 256), F32),
            pltpu.VMEM((256, 256), F32),
            pltpu.VMEM((256, 256), F32),
            pltpu.VMEM((2, 3, 4, 2, 4, 8, 256), BF16),
            pltpu.VMEM((2, 3, 256, 256), BF16),
            pltpu.VMEM((2, 48, 256), F32),
            pltpu.VMEM((2, 2, 4, 8, 3, 8, 256), BF16),
            pltpu.VMEM((2, 2, 2, 8, 3, 8, 256), BF16),
            pltpu.VMEM((2, 2, 8, 3, 8, 256), BF16),
            pltpu.VMEM((2, 2, 8, 3, 8, 256), BF16),
            pltpu.VMEM((2, 8, 3, 8, 256), F32),
            pltpu.VMEM((2, 8, 6, 8, 256), BF16),
            pltpu.VMEM((2, 7, 6, 8, 256), BF16),
            *e_scratch(2),
            *e_scratch(1),
            pltpu.VMEM((256, 256), F32),
            pltpu.VMEM((48, 256), F32),
            pltpu.SemaphoreType.DMA((6,)),
            pltpu.SemaphoreType.DMA((2, 4)),
            pltpu.SemaphoreType.DMA((11, 2)),
            pltpu.SemaphoreType.DMA((11, 2)),
        ],
        compiler_params=pltpu.CompilerParams(
            collective_id=0, has_side_effects=True, vmem_limit_bytes=40 * 1024 * 1024),
    )(
        stored_inverse.reshape(6, 3, 256, 256),
        panel_first.reshape(3, 2, 8, 256),
        panel_second.reshape(3, 2, 8, 256),
        panel_link, inv_first, inv_second,
        struct_first.reshape(1, -1), struct_second.reshape(1, -1),
    )
    return c1.reshape(6, 1, 8, 256), c2.reshape(6, 1, 8, 256), d1, lk, d2


def solution(mesh):
    return jax.shard_map(
        body,
        mesh=mesh,
        in_specs=(P(None, "row", None, "col", None, None), P(None, "row", "col", None), P(None, "row", "col", None),
                  P(), P(), P(), P(), P()),
        out_specs=(P(None, "row", "col", None), P(None, "row", "col", None), P("col", None), P("col", None), P("col", None)),
        check_vma=False,
    )
```

time: 964 us -> 85.4 us (0.09)
  waiting for transfers between devices: 844 us -> 0 us
  blocking collectives: 77.8 us -> 0 us
  Pallas kernels: 0 us -> 74.1 us
  matrix products: 16.8 us -> 0 us
  between operations: 13.9 us -> 0.66 us
    reduce_scatter x2 -> x0, waiting for transfers between devices: 435 us -> none  [column_sums(): lax.psum_scatter(jnp.einsum('abij,bjl->ial', stored, factors, preferred_e...]
    psum x2 -> x0, waiting for transfers between devices: 409 us -> none  [the longest x1 277 us: body(): lax.psum((first_term, top_term, second_term), ('row', 'col'))]
    all_gather x2 -> x0, blocking collectives: 77.8 us -> none  [spread_factor(): gathered = lax.all_gather(factor_part, 'col', axis=1, tiled=True)]
    pallas_call x0 -> x1, Pallas kernels: none -> 74.1 us  [body(): pl.pallas_call(kernel, out_shape=[jax.ShapeDtypeStruct((6, 8, 256), F32)]...]
    dot_general x13 -> x0, matrix products: 16.8 us -> none  [the longest x2 5.98 us: column_sums(): jnp.einsum('abij,bjl->ial', stored, factors, preferred_element_type=jnp.f...]
  transfers between devices with their start and end apart: 4 -> 0, of which waited for: 4 -> 0; matrix products, arithmetic and copies ran while one was open for 1% -> 0% of each run, Pallas kernels for 0% -> 0%
where the time goes in v1:
time: 85.4 us; the launch traced here: 85 us
  Pallas kernels  74.1 us (87%)
  local copies, waits for them, and re-layouts  10.3 us (12%)
    pallas_call x1, Pallas kernels, body(): pl.pallas_call(kernel, out_shape=[jax.ShapeDtypeStruct((6, 8, 256), F32)]...  74.1 us
    unnamed x21, local copies, waits for them, and re-layouts  10.3 us

profile of v1, /device:TPU:1, one launch (start us, length us, event | category | flops | bytes accessed | tf_op | source)
XLA Modules:
  0.0 85.0 jit_solution(4476991404248771192)
XLA Ops:
  0.6 0.0 copy-start
  0.6 1.7 %copy-done = bf16[6,1,3,1,256,256]{5,4,3,2,1,0:T(8,128)(2,1)S(1)} copy-done((bf16[6,1,3,1,256,256]{5,4,3,2,1,0:T(8,128)(2,1)S(1)}, bf16[6,1,3,1,256,256]{5,4,3,2,1,0:T(8,128)(2,1)}, u32[]{:S(2)}) %copy-start) | copy-done | bytes 2359320
  2.3 0.0 copy-start.1
  2.3 0.9 %copy-done.1 = f32[256,256]{1,0:T(8,128)S(1)} copy-done((f32[256,256]{1,0:T(8,128)S(1)}, f32[256,256]{1,0:T(8,128)}, u32[]{:S(2)}) %copy-start.1) | copy-done | bytes 262168
  3.3 0.0 copy-start.2
  3.3 0.9 %copy-done.2 = f32[256,256]{1,0:T(8,128)S(1)} copy-done((f32[256,256]{1,0:T(8,128)S(1)}, f32[256,256]{1,0:T(8,128)}, u32[]{:S(2)}) %copy-start.2) | copy-done | bytes 262168
  4.2 0.0 copy-start.3
  4.2 0.9 %copy-done.3 = bf16[256,256]{1,0:T(8,128)(2,1)S(1)} copy-done((bf16[256,256]{1,0:T(8,128)(2,1)S(1)}, bf16[256,256]{1,0:T(8,128)(2,1)}, u32[]{:S(2)}) %copy-start.3) | copy-done | bytes 131096
  5.1 0.0 copy-start.4
  5.1 0.7 copy-done.4
  5.8 0.0 copy-start.5
  5.8 0.7 copy-done.5
  6.6 0.0 copy-start.6
  6.6 0.7 copy-done.6
  7.2 0.0 copy-start.7
  7.2 0.7 copy-done.7
  7.9 74.1 %shard_map.119 = (f32[6,8,256]{2,1,0:T(8,128)S(1)}, f32[6,8,256]{2,1,0:T(8,128)S(1)}, f32[8,256]{1,0:T(8,128)S(1)}, f32[8,256]{1,0:T(8,128)S(1)}, f32[8,256]{1,0:T(8,128)S(1)}) custom-call(bf16[6,3,256,256]{3,2,1,0:T(8,128)(2,1)S(1)} %bitcast.11, bf16[3,2,8,256]{3,2,1,0:T(8,128)(2,1)S(1)} %bitcast.14, bf16[3,2,8,256]{3,2,1,0:T(8,128)(2,1)S(1)} %bitcast.15, ...), custom_call_target="tpu_custom_call" | custom-call | tf_op jit(solution)/shard_map/pallas_call | solution.py:292
  82.0 0.6 copy.20
  82.6 0.6 copy.21
  83.2 0.6 copy.22
  83.8 0.6 copy.23
  84.4 0.6 copy.24
Async XLA Ops:
  0.6 1.7 %copy-start = (bf16[6,1,3,1,256,256]{5,4,3,2,1,0:T(8,128)(2,1)S(1)}, bf16[6,1,3,1,256,256]{5,4,3,2,1,0:T(8,128)(2,1)}, u32[]{:S(2)}) copy-start(bf16[6,1,3,1,256,256]{5,4,3,2,1,0:T(8,128)(2,1)} %param.8) | copy-start | bytes 7077892
  2.3 0.9 %copy-start.1 = (f32[256,256]{1,0:T(8,128)S(1)}, f32[256,256]{1,0:T(8,128)}, u32[]{:S(2)}) copy-start(f32[256,256]{1,0:T(8,128)} %inv1_hbm.1) | copy-start | bytes 786436
  3.3 0.9 %copy-start.2 = (f32[256,256]{1,0:T(8,128)S(1)}, f32[256,256]{1,0:T(8,128)}, u32[]{:S(2)}) copy-start(f32[256,256]{1,0:T(8,128)} %inv2_hbm.1) | copy-start | bytes 786436
  4.2 0.9 %copy-start.3 = (bf16[256,256]{1,0:T(8,128)(2,1)S(1)}, bf16[256,256]{1,0:T(8,128)(2,1)}, u32[]{:S(2)}) copy-start(bf16[256,256]{1,0:T(8,128)(2,1)} %link_hbm.1) | copy-start | bytes 393220
  5.1 0.7 copy-start.4
  5.8 0.7 copy-start.5
  6.6 0.7 copy-start.6
  7.2 0.7 copy-start.7

commit v2 on v1

v2 whole, which is shorter than its diff:
```python
import jax
import jax.numpy as jnp
from jax import lax
from jax.experimental import pallas as pl
from jax.experimental.pallas import tpu as pltpu
from jax.sharding import PartitionSpec as P

NX, NY, NZ = 4, 8, 8
F32, BF16 = jnp.float32, jnp.bfloat16
precise = lax.Precision.HIGHEST


def dev(row, col):
    return {"row": row, "col": col}


def fdot(a, b):
    return jnp.dot(a, b, preferred_element_type=F32, precision=precise)


def tdot(a, b):
    return lax.dot_general(a, b, (((0,), (0,)), ((), ())), preferred_element_type=F32, precision=precise)


def wait_bytes(ref, sem):
    pltpu.make_async_copy(ref, ref, sem).wait()


def listed(struct_ref, block):
    hit = jnp.where(struct_ref[...] == block, 1.0, 0.0)
    return jnp.max(hit, axis=1, keepdims=True)


def kernel(
    s_hbm, p1_hbm, p2_hbm, link_hbm, inv1_hbm, inv2_hbm, st1_hbm, st2_hbm,
    out,
    st1, st2, s_v, link_v, inv_v, wide, tall, gram1, gram2, rows_z, masked, fac_t, raw, fac,
    part_out, part_in, summed, z_out, z_in,
    ea_own, ea_twin, ea_out, ea_in, ea_z, ea_zin, ea_y, ea_yin, ea_sum,
    eb_own, eb_twin, eb_out, eb_in, eb_z, eb_zin, eb_y, eb_yin, eb_sum, rest, carry,
    load_sem, a_send, send_sem, recv_sem,
):
    row, col = lax.axis_index("row"), lax.axis_index("col")
    col1, col2 = out.at[pl.ds(0, 6)], out.at[pl.ds(6, 6)]
    diag1, link, diag2 = out.at[12], out.at[13], out.at[14]
    y, core = lax.div(row, 2), lax.rem(row, 2)
    z, x = lax.div(col, NX), lax.rem(col, NX)
    quad = lax.rem(y, 4)

    loads = [
        pltpu.make_async_copy(p1_hbm, rows_z.at[z, 0], load_sem.at[0]),
        pltpu.make_async_copy(p2_hbm, rows_z.at[z, 1], load_sem.at[1]),
        pltpu.make_async_copy(inv1_hbm, inv_v.at[0], load_sem.at[2]),
        pltpu.make_async_copy(inv2_hbm, inv_v.at[1], load_sem.at[3]),
        pltpu.make_async_copy(link_hbm, link_v, load_sem.at[4]),
        pltpu.make_async_copy(st1_hbm, st1, load_sem.at[6]),
        pltpu.make_async_copy(st2_hbm, st2, load_sem.at[7]),
        pltpu.make_async_copy(s_hbm, s_v, load_sem.at[5]),
    ]
    for load in loads:
        load.start()

    barrier = pltpu.get_barrier_semaphore()

    def greet(r, c):
        pl.semaphore_signal(barrier, inc=1, device_id=dev(r, c), device_id_type=pl.DeviceIdType.MESH)

    src_row = lax.rem(col, 16)
    for slot in range(4):
        src_col = 4 * (2 * quad + core) + slot
        me = jnp.logical_and(src_row == row, src_col == col)

        @pl.when(jnp.logical_not(me))
        def _():
            greet(src_row, src_col)

    for d in range(1, NZ):
        greet(row, 4 * lax.rem(z + d, NZ) + x)
    for d in range(1, NX):
        greet(row, 4 * z + lax.rem(x + d, NX))
    for d in range(1, NY):
        greet(2 * lax.rem(y + d, NY) + core, col)
    twin = 2 * y + 1 - core
    greet(twin, col)

    targets = []
    others = 3 + 7 + 7 + 1
    for zhi in range(2):
        for k in range(2):
            r_t = 2 * (lax.div(z, 2) + 4 * k) + lax.rem(z, 2)
            c_t = row + 16 * zhi
            me = jnp.logical_and(r_t == row, c_t == col)
            others = others + jnp.where(me, 0, 1)
            targets.append((zhi, k, r_t, c_t, me))
    loads[0].wait()
    loads[1].wait()
    pl.semaphore_wait(barrier, others)

    spot_a = raw.at[:, :, lax.div(col, 8), lax.rem(lax.div(col, 4), 2), lax.rem(col, 4)]

    def stage_a(zhi, k, r_t, c_t):
        return pltpu.make_async_remote_copy(
            rows_z.at[z, :, :, zhi], spot_a, a_send.at[2 * zhi + k], recv_sem.at[0, 0],
            device_id=dev(r_t, c_t), device_id_type=pl.DeviceIdType.MESH)

    for zhi, k, r_t, c_t, me in targets:
        @pl.when(jnp.logical_not(me))
        def _():
            stage_a(zhi, k, r_t, c_t).start()

        @pl.when(me)
        def _():
            pltpu.make_async_copy(rows_z.at[z, :, :, zhi], spot_a, recv_sem.at[0, 0]).start()

    def remote(src, dst, stage, sn, r, c):
        pltpu.make_async_remote_copy(
            src, dst, send_sem.at[stage, sn], recv_sem.at[stage, sn],
            device_id=dev(r, c), device_id_type=pl.DeviceIdType.MESH).start()

    wait_bytes(raw.at[:, :, quad, core], recv_sem.at[0, 0])
    for sn in range(2):
        spot = raw.at[sn, :, quad, core]
        for d in (2 + 4 * sn, 1, 7):
            remote(spot, spot, 1, sn, 2 * lax.rem(y + d, NY) + core, col)
    for d in (4, 3, 5, 2, 6, 1, 7):
        remote(rows_z.at[z], rows_z.at[z], 5, 0, row, 4 * lax.rem(z + d, NZ) + x)
    for load in loads[2:-1]:
        load.wait()
    wide[...] = fdot(link_v[...].astype(F32), inv_v[1])
    for sn in range(2):
        wait_bytes(raw.at[sn, :, pl.ds(0, 3), core], recv_sem.at[1, sn])
        spot = raw.at[sn, :, :, core]
        remote(spot, spot, 2, sn, twin, col)
    loads[-1].wait()

    structs = (st1, st2)
    uppers = [inv_v[sn].astype(BF16) for sn in range(2)]
    lowers = [(inv_v[sn] - uppers[sn].astype(F32)).astype(BF16) for sn in range(2)]

    def times_inverse(rows, sn):
        return (jnp.dot(rows, uppers[sn], preferred_element_type=F32)
                + jnp.dot(rows, lowers[sn], preferred_element_type=F32))

    for sn in range(2):
        wait_bytes(raw.at[sn, :, :, core], recv_sem.at[2, sn])
        for b in range(3):
            rows = raw[sn, b].astype(F32).reshape(256, 256).astype(BF16)
            fac[sn, b] = (times_inverse(rows, sn) * listed(structs[sn], b * 32 + col)).astype(BF16)
        for half in range(2):
            def block_row(step, _):
                a = 3 * half + step
                total = jnp.dot(s_v[a, 0], fac[sn, 0], preferred_element_type=F32)
                total += jnp.dot(s_v[a, 1], fac[sn, 1], preferred_element_type=F32)
                total += jnp.dot(s_v[a, 2], fac[sn, 2], preferred_element_type=F32)
                for xd in range(NX):
                    for zd in range(NZ):
                        at = 8 * (4 * zd + xd)
                        part_out[sn, half, xd, zd, step] = total[at:at + 8, :].astype(BF16)
                return 0

            lax.fori_loop(0, 3, block_row, 0)
            for d in (2, 1, 3):
                to = lax.rem(x + d, NX)
                remote(part_out.at[sn, half, to], part_in.at[sn, half, d - 1], 3 + half, sn, row, 4 * z + to)

    wait_bytes(rows_z.at[pl.ds(0, 7)], recv_sem.at[5, 0])
    for sn in range(2):
        for block in range(6):
            masked[:, block] = rows_z[:, sn, block // 2, block % 2].astype(F32) * listed(structs[sn], block * 16 + row)
        product = times_inverse(masked[...].reshape(384, 256).astype(BF16), sn)
        fac_t[sn] = product.T.astype(BF16)
    tall[...] = wide[...].T

    def spread_rows(to, m, matrix):
        for xd in range(NX):
            for zd in range(NZ):
                at = 8 * (4 * zd + xd)
                for lanes in range(2):
                    to[lanes, xd, zd, m] = matrix[at:at + 8, 128 * lanes:128 * lanes + 128]

    groups = ((ea_own, ea_twin, ea_out, ea_in, ea_z, ea_zin, ea_y, ea_yin, ea_sum),
              (eb_own, eb_twin, eb_out, eb_in, eb_z, eb_zin, eb_y, eb_yin, eb_sum))
    for sn in range(2):
        for half in range(2):
            wait_bytes(part_in.at[sn, half], recv_sem.at[3 + half, sn])
            total = part_out[sn, half, x].astype(F32)
            for d in range(3):
                total += part_in[sn, half, d].astype(F32)
            summed[:, 3 * half:3 * half + 3] = total
            z_out[sn, :, 3 * half:3 * half + 3] = total.astype(BF16)
        for d in (4, 3, 5, 2, 6, 1, 7):
            to = lax.rem(z + d, NZ)
            remote(z_out.at[sn, to], z_in.at[sn, d - 1], 7, sn, row, 4 * to + x)
        high = summed[...].reshape(384, 256).astype(BF16)
        low = (summed[...].reshape(384, 256) - high.astype(F32)).astype(BF16)

        def part_sum(which):
            return -(jnp.dot(fac_t[which], high, preferred_element_type=F32)
                     + jnp.dot(fac_t[which], low, preferred_element_type=F32))

        g_own, g_twin, g_out, g_in = groups[sn][:4]
        if sn == 0:
            first = part_sum(0)
            top_t = part_sum(1)
            top = top_t.T
            spread_rows(g_own, 0, first)
            spread_rows(g_own, 1, top)
        else:
            spread_rows(g_own, 0, part_sum(1) + rest[...])
        remote(g_own.at[1 - core], g_twin, 6, sn, twin, col)
        if sn == 0:
            rest[...] = fdot(tall[...], fdot(first, wide[...]) - top) - fdot(top_t, wide[...])
        wait_bytes(g_twin, recv_sem.at[6, sn])
        g_out[...] = (g_own[core] + g_twin[...]).astype(BF16)
        for d in (2, 1, 3):
            to = lax.rem(x + d, NX)
            remote(g_out.at[to], g_in.at[d - 1], 8, sn, row, 4 * z + to)

    for g in range(2):
        g_out, g_in, g_z, g_zin = groups[g][2:6]
        wait_bytes(g_in, recv_sem.at[8, g])
        total = g_out[x].astype(F32)
        for d in range(3):
            total += g_in[d].astype(F32)
        g_z[...] = total.astype(BF16)
        for d in (4, 3, 5, 2, 6, 1, 7):
            to = lax.rem(z + d, NZ)
            remote(g_z.at[to], g_zin.at[d - 1], 9, g, row, 4 * to + x)
    gram1[...] = tdot(inv_v[0], inv_v[0])
    gram2[...] = tdot(inv_v[1], inv_v[1]) + fdot(tall[...], fdot(gram1[...], wide[...]))

    def z_total(sn):
        wait_bytes(z_in.at[sn], recv_sem.at[7, sn])
        total = z_out[sn, z].astype(F32)
        for d in range(7):
            total += z_in[sn, d].astype(F32)
        return total

    total = z_total(0)
    for block in range(6):
        col1[block] = total[block] * (-listed(st1, block * 16 + row))
    carry[...] = fdot(col1[...].reshape(48, 256), wide[...])

    for g in range(2):
        g_z, g_zin, g_y, g_yin = groups[g][4:8]
        wait_bytes(g_zin, recv_sem.at[9, g])
        total = g_z[z].astype(F32)
        for d in range(7):
            total += g_zin[d].astype(F32)
        g_y[...] = total
        for d in (4, 3, 5, 2, 6, 1, 7):
            remote(g_y, g_yin.at[d - 1], 10, g, 2 * lax.rem(y + d, NY) + core, col)

    total = z_total(1).reshape(48, 256) + carry[...]
    for block in range(6):
        col2[block] = total[8 * block:8 * block + 8, :] * (-listed(st2, block * 16 + row))

    for g in range(2):
        g_y, g_yin, g_sum = groups[g][6:9]
        wait_bytes(g_yin, recv_sem.at[10, g])
        total = g_y[...]
        for d in range(7):
            total += g_yin[d]
        g_sum[core] = total
        remote(g_sum.at[core], g_sum.at[core], 11, g, twin, col)
    for g in range(2):
        wait_bytes(groups[g][8].at[core], recv_sem.at[11, g])

    at = pl.multiple_of(8 * col, 8)

    def whole(g_sum, m):
        return jnp.concatenate([g_sum[0, m], g_sum[1, m]], axis=1)

    diag1[...] = gram1[pl.ds(at, 8), :] - whole(ea_sum, 0)
    link[...] = -(whole(ea_sum, 1) + fdot(diag1[...], wide[...]))
    diag2[...] = gram2[pl.ds(at, 8), :] - whole(eb_sum, 0)

    for zhi, k, r_t, c_t, me in targets:
        @pl.when(jnp.logical_not(me))
        def _():
            stage_a(zhi, k, r_t, c_t).wait_send()

    wait_bytes(rows_z.at[pl.ds(0, 7)], send_sem.at[5, 0])
    for sn in range(2):
        wait_bytes(raw.at[sn, :, pl.ds(0, 3), core], send_sem.at[1, sn])
        wait_bytes(raw.at[sn, :, :, core], send_sem.at[2, sn])
        for half in range(2):
            wait_bytes(part_in.at[sn, half], send_sem.at[3 + half, sn])
        wait_bytes(z_in.at[sn], send_sem.at[7, sn])
        wait_bytes(groups[sn][1], send_sem.at[6, sn])
        wait_bytes(groups[sn][3], send_sem.at[8, sn])
        wait_bytes(groups[sn][5], send_sem.at[9, sn])
        wait_bytes(groups[sn][7], send_sem.at[10, sn])
        wait_bytes(groups[sn][8].at[core], send_sem.at[11, sn])


def body(stored_inverse, panel_first, panel_second, panel_link, inv_first, inv_second, struct_first, struct_second):
    anywhere = pl.BlockSpec(memory_space=pl.ANY)
    vmem = pl.BlockSpec(memory_space=pltpu.VMEM)

    def e_scratch(n):
        return [
            pltpu.VMEM((2, 4, 8, n, 8, 128), F32), pltpu.VMEM((4, 8, n, 8, 128), F32),
            pltpu.VMEM((4, 8, n, 8, 128), BF16), pltpu.VMEM((3, 8, n, 8, 128), BF16),
            pltpu.VMEM((8, n, 8, 128), BF16), pltpu.VMEM((7, n, 8, 128), BF16),
            pltpu.VMEM((n, 8, 128), F32), pltpu.VMEM((7, n, 8, 128), F32), pltpu.VMEM((2, n, 8, 128), F32),
        ]

    out = pl.pallas_call(
        kernel,
        out_shape=jax.ShapeDtypeStruct((15, 8, 256), F32),
        in_specs=[anywhere] * 8,
        out_specs=vmem,
        scratch_shapes=[
            pltpu.VMEM(struct_first.reshape(1, -1).shape, jnp.int32),
            pltpu.VMEM(struct_second.reshape(1, -1).shape, jnp.int32),
            pltpu.VMEM((6, 3, 256, 256), BF16),
            pltpu.VMEM((256, 256), BF16),
            pltpu.VMEM((2, 256, 256), F32),
            pltpu.VMEM((256, 256), F32),
            pltpu.VMEM((256, 256), F32),
            pltpu.VMEM((256, 256), F32),
            pltpu.VMEM((256, 256), F32),
            pltpu.VMEM((8, 2, 3, 2, 8, 256), BF16),
            pltpu.VMEM((8, 6, 8, 256), F32),
            pltpu.VMEM((2, 256, 384), BF16),
            pltpu.VMEM((2, 3, 4, 2, 4, 8, 256), BF16),
            pltpu.VMEM((2, 3, 256, 256), BF16),
            pltpu.VMEM((2, 2, 4, 8, 3, 8, 256), BF16),
            pltpu.VMEM((2, 2, 3, 8, 3, 8, 256), BF16),
            pltpu.VMEM((8, 6, 8, 256), F32),
            pltpu.VMEM((2, 8, 6, 8, 256), BF16),
            pltpu.VMEM((2, 7, 6, 8, 256), BF16),
            *e_scratch(2),
            *e_scratch(1),
            pltpu.VMEM((256, 256), F32),
            pltpu.VMEM((48, 256), F32),
            pltpu.SemaphoreType.DMA((8,)),
            pltpu.SemaphoreType.DMA((4,)),
            pltpu.SemaphoreType.DMA((12, 2)),
            pltpu.SemaphoreType.DMA((12, 2)),
        ],
        compiler_params=pltpu.CompilerParams(
            collective_id=0, has_side_effects=True, vmem_limit_bytes=40 * 1024 * 1024),
    )(
        *[pltpu.with_memory_space_constraint(v, pltpu.HBM) for v in (
            stored_inverse.reshape(6, 3, 256, 256),
            panel_first.reshape(3, 2, 8, 256),
            panel_second.reshape(3, 2, 8, 256),
            panel_link, inv_first, inv_second,
            struct_first.reshape(1, -1), struct_second.reshape(1, -1),
        )])
    c1, c2, d1, lk, d2 = out[:6], out[6:12], out[12], out[13], out[14]
    return c1.reshape(6, 1, 8, 256), c2.reshape(6, 1, 8, 256), d1, lk, d2


def solution(mesh):
    return jax.shard_map(
        body,
        mesh=mesh,
        in_specs=(P(None, "row", None, "col", None, None), P(None, "row", "col", None), P(None, "row", "col", None),
                  P(), P(), P(), P(), P()),
        out_specs=(P(None, "row", "col", None), P(None, "row", "col", None), P("col", None), P("col", None), P("col", None)),
        check_vma=False,
    )
```

time: 85.4 us -> 71.2 us (0.83)
  local copies, waits for them, and re-layouts: 10.3 us -> 1.25 us
  Pallas kernels: 74.1 us -> 69.2 us
    unnamed x21 -> x1, local copies, waits for them, and re-layouts: 10.3 us -> 0.64 us
    pallas_call x1, Pallas kernels: 74.1 us -> 69.2 us  [body(): pl.pallas_call(kernel, out_shape=jax.ShapeDtypeStruct((15, 8, 256), F32),...]
where the time goes in v2:
time: 71.2 us; the launch traced here: 71.1 us
  Pallas kernels  69.2 us (97%)
  local copies, waits for them, and re-layouts  1.25 us (2%)
    pallas_call x1, Pallas kernels, body(): pl.pallas_call(kernel, out_shape=jax.ShapeDtypeStruct((15, 8, 256), F32),...  69.2 us

profile of v2, /device:TPU:1, one launch (start us, length us, event | category | flops | bytes accessed | tf_op | source)
XLA Modules:
  0.0 71.1 jit_solution(15463134813614568006)
XLA Ops:
  0.6 69.2 %shard_map.119 = f32[15,8,256]{2,1,0:T(8,128)S(1)} custom-call(bf16[6,3,256,256]{3,2,1,0:T(8,128)(2,1)} %bitcast.19, bf16[3,2,8,256]{3,2,1,0:T(8,128)(2,1)} %bitcast.20, bf16[3,2,8,256]{3,2,1,0:T(8,128)(2,1)} %bitcast.21, bf16[256,256]{1,0:T(8,128)(2,1)} %link_hbm.1, f32[256,256]{1,0:T(8,128)} %inv1_hbm.1, f32[256,256]{1,0:T(8,128)} %inv2_hbm.1, ...), custom_call_target="tpu_custom_call" | custom-call | tf_op jit(solution)/shard_map/pallas_call | solution.py:309
  69.8 0.6 slice_bitcast_fusion.2
  70.4 0.6 slice_bitcast_fusion

commit v3 on v2

--- a/solution.py
+++ b/solution.py
@@ -34,8 +34,8 @@
 def kernel(
     s_hbm, p1_hbm, p2_hbm, link_hbm, inv1_hbm, inv2_hbm, st1_hbm, st2_hbm,
     out,
-    st1, st2, s_v, link_v, inv_v, wide, tall, gram1, gram2, rows_z, masked, fac_t, raw, fac,
-    part_out, part_in, summed, z_out, z_in,
+    st1, st2, s_v, link_v, inv_v, wide, tall, gram1, gram2, p_v, rows_z, rows_x, ordered, fac_t, raw, fac,
+    q_out, q_in, q_x, q_xin, part_out, part_in, summed, z_out, z_in,
     ea_own, ea_twin, ea_out, ea_in, ea_z, ea_zin, ea_y, ea_yin, ea_sum,
     eb_own, eb_twin, eb_out, eb_in, eb_z, eb_zin, eb_y, eb_yin, eb_sum, rest, carry,
     load_sem, a_send, send_sem, recv_sem,
@@ -48,8 +48,8 @@
     quad = lax.rem(y, 4)
 
     loads = [
-        pltpu.make_async_copy(p1_hbm, rows_z.at[z, 0], load_sem.at[0]),
-        pltpu.make_async_copy(p2_hbm, rows_z.at[z, 1], load_sem.at[1]),
+        pltpu.make_async_copy(p1_hbm, p_v.at[0], load_sem.at[0]),
+        pltpu.make_async_copy(p2_hbm, p_v.at[1], load_sem.at[1]),
         pltpu.make_async_copy(inv1_hbm, inv_v.at[0], load_sem.at[2]),
         pltpu.make_async_copy(inv2_hbm, inv_v.at[1], load_sem.at[3]),
         pltpu.make_async_copy(link_hbm, link_v, load_sem.at[4]),
@@ -92,8 +92,19 @@
             me = jnp.logical_and(r_t == row, c_t == col)
             others = others + jnp.where(me, 0, 1)
             targets.append((zhi, k, r_t, c_t, me))
-    loads[0].wait()
-    loads[1].wait()
+    for load in loads[:-1]:
+        load.wait()
+    structs = (st1, st2)
+    uppers = [inv_v[sn].astype(BF16) for sn in range(2)]
+    for sn in range(2):
+        lower = (inv_v[sn] - uppers[sn].astype(F32)).astype(BF16)
+        rows = jnp.concatenate([
+            p_v[sn, block // 2, block % 2].astype(F32) * listed(structs[sn], block * 16 + row) for block in range(6)
+        ], axis=0).astype(BF16)
+        product = (jnp.dot(rows, uppers[sn], preferred_element_type=F32)
+                   + jnp.dot(rows, lower, preferred_element_type=F32))
+        rows_z[z, sn] = product.reshape(3, 2, 8, 256).astype(BF16)
+    rows_x[x] = rows_z[z, 1]
     pl.semaphore_wait(barrier, others)
 
     spot_a = raw.at[:, :, lax.div(col, 8), lax.rem(lax.div(col, 4), 2), lax.rem(col, 4)]
@@ -124,8 +135,8 @@
             remote(spot, spot, 1, sn, 2 * lax.rem(y + d, NY) + core, col)
     for d in (4, 3, 5, 2, 6, 1, 7):
         remote(rows_z.at[z], rows_z.at[z], 5, 0, row, 4 * lax.rem(z + d, NZ) + x)
-    for load in loads[2:-1]:
-        load.wait()
+    for d in (2, 1, 3):
+        remote(rows_x.at[x], rows_x.at[x], 14, 0, row, 4 * z + lax.rem(x + d, NX))
     wide[...] = fdot(link_v[...].astype(F32), inv_v[1])
     for sn in range(2):
         wait_bytes(raw.at[sn, :, pl.ds(0, 3), core], recv_sem.at[1, sn])
@@ -133,20 +144,11 @@
         remote(spot, spot, 2, sn, twin, col)
     loads[-1].wait()
 
-    structs = (st1, st2)
-    uppers = [inv_v[sn].astype(BF16) for sn in range(2)]
-    lowers = [(inv_v[sn] - uppers[sn].astype(F32)).astype(BF16) for sn in range(2)]
-
-    def times_inverse(rows, sn):
-        return (jnp.dot(rows, uppers[sn], preferred_element_type=F32)
-                + jnp.dot(rows, lowers[sn], preferred_element_type=F32))
-
     for sn in range(2):
         wait_bytes(raw.at[sn, :, :, core], recv_sem.at[2, sn])
         for b in range(3):
-            rows = raw[sn, b].astype(F32).reshape(256, 256).astype(BF16)
-            fac[sn, b] = (times_inverse(rows, sn) * listed(structs[sn], b * 32 + col)).astype(BF16)
-        for half in range(2):
+            fac[sn, b] = raw[sn, b].astype(F32).reshape(256, 256).astype(BF16)
+        for half in ((0, 1) if sn == 0 else (1, 0)):
             def block_row(step, _):
                 a = 3 * half + step
                 total = jnp.dot(s_v[a, 0], fac[sn, 0], preferred_element_type=F32)
@@ -155,20 +157,30 @@
                 for xd in range(NX):
                     for zd in range(NZ):
                         at = 8 * (4 * zd + xd)
-                        part_out[sn, half, xd, zd, step] = total[at:at + 8, :].astype(BF16)
+                        piece = total[at:at + 8, :].astype(BF16)
+                        if sn and half:
+                            q_out[zd, xd, step] = piece
+                        else:
+                            part_out[2 * sn + half, xd, zd, step] = piece
                 return 0
 
             lax.fori_loop(0, 3, block_row, 0)
-            for d in (2, 1, 3):
-                to = lax.rem(x + d, NX)
-                remote(part_out.at[sn, half, to], part_in.at[sn, half, d - 1], 3 + half, sn, row, 4 * z + to)
+            if sn and half:
+                for d in (4, 3, 5, 2, 6, 1, 7):
+                    to = lax.rem(z + d, NZ)
+                    remote(q_out.at[to], q_in.at[d - 1], 12, 0, row, 4 * to + x)
+            else:
+                n = 2 * sn + half
+                for d in (2, 1, 3):
+                    to = lax.rem(x + d, NX)
+                    remote(part_out.at[n, to], part_in.at[n, d - 1], 3 + half, sn, row, 4 * z + to)
 
     wait_bytes(rows_z.at[pl.ds(0, 7)], recv_sem.at[5, 0])
+    wait_bytes(rows_x.at[pl.ds(0, 3)], recv_sem.at[14, 0])
     for sn in range(2):
         for block in range(6):
-            masked[:, block] = rows_z[:, sn, block // 2, block % 2].astype(F32) * listed(structs[sn], block * 16 + row)
-        product = times_inverse(masked[...].reshape(384, 256).astype(BF16), sn)
-        fac_t[sn] = product.T.astype(BF16)
+            ordered[block // 3, :, block % 3] = rows_z[:, sn, block // 2, block % 2].astype(F32)
+        fac_t[sn] = ordered[...].reshape(384, 256).T.astype(BF16)
     tall[...] = wide[...].T
 
     def spread_rows(to, m, matrix):
@@ -181,22 +193,26 @@
     groups = ((ea_own, ea_twin, ea_out, ea_in, ea_z, ea_zin, ea_y, ea_yin, ea_sum),
               (eb_own, eb_twin, eb_out, eb_in, eb_z, eb_zin, eb_y, eb_yin, eb_sum))
     for sn in range(2):
-        for half in range(2):
-            wait_bytes(part_in.at[sn, half], recv_sem.at[3 + half, sn])
-            total = part_out[sn, half, x].astype(F32)
+        for half in range(2 - sn):
+            n = 2 * sn + half
+            wait_bytes(part_in.at[n], recv_sem.at[3 + half, sn])
+            total = part_out[n, x].astype(F32)
             for d in range(3):
-                total += part_in[sn, half, d].astype(F32)
-            summed[:, 3 * half:3 * half + 3] = total
-            z_out[sn, :, 3 * half:3 * half + 3] = total.astype(BF16)
-        for d in (4, 3, 5, 2, 6, 1, 7):
-            to = lax.rem(z + d, NZ)
-            remote(z_out.at[sn, to], z_in.at[sn, d - 1], 7, sn, row, 4 * to + x)
-        high = summed[...].reshape(384, 256).astype(BF16)
-        low = (summed[...].reshape(384, 256) - high.astype(F32)).astype(BF16)
+                total += part_in[n, d].astype(F32)
+            summed[half] = total
+            z_out[n] = total.astype(BF16)
+            for d in (4, 3, 5, 2, 6, 1, 7):
+                to = lax.rem(z + d, NZ)
+                remote(z_out.at[n, to], z_in.at[n, d - 1], 7 + 8 * half, sn, row, 4 * to + x)
+        depth = 384 - 192 * sn
+        sums = (summed[...] if sn == 0 else summed[0]).reshape(depth, 256)
+        high = sums.astype(BF16)
+        low = (sums - high.astype(F32)).astype(BF16)
 
         def part_sum(which):
-            return -(jnp.dot(fac_t[which], high, preferred_element_type=F32)
-                     + jnp.dot(fac_t[which], low, preferred_element_type=F32))
+            factor = fac_t[which, :, 0:depth]
+            return -(jnp.dot(factor, high, preferred_element_type=F32)
+                     + jnp.dot(factor, low, preferred_element_type=F32))
 
         g_own, g_twin, g_out, g_in = groups[sn][:4]
         if sn == 0:
@@ -206,7 +222,17 @@
             spread_rows(g_own, 0, first)
             spread_rows(g_own, 1, top)
         else:
-            spread_rows(g_own, 0, part_sum(1) + rest[...])
+            second = part_sum(1) + rest[...]
+            wait_bytes(q_in, recv_sem.at[12, 0])
+            total = q_out[z].astype(F32)
+            for d in range(7):
+                total += q_in[d].astype(F32)
+            q_x[...] = total.astype(BF16)
+            for d in (2, 1, 3):
+                to = lax.rem(x + d, NX)
+                remote(q_x.at[to], q_xin.at[d - 1], 13, 0, row, 4 * z + to)
+            late = jnp.stack([rows_x[:, block // 2, block % 2].astype(F32) for block in (3, 4, 5)], axis=1)
+            spread_rows(g_own, 0, second - tdot(late.reshape(96, 256), total.reshape(96, 256)))
         remote(g_own.at[1 - core], g_twin, 6, sn, twin, col)
         if sn == 0:
             rest[...] = fdot(tall[...], fdot(first, wide[...]) - top) - fdot(top_t, wide[...])
@@ -229,16 +255,18 @@
     gram1[...] = tdot(inv_v[0], inv_v[0])
     gram2[...] = tdot(inv_v[1], inv_v[1]) + fdot(tall[...], fdot(gram1[...], wide[...]))
 
-    def z_total(sn):
-        wait_bytes(z_in.at[sn], recv_sem.at[7, sn])
-        total = z_out[sn, z].astype(F32)
+    def z_total(n, stage, sn):
+        wait_bytes(z_in.at[n], recv_sem.at[stage, sn])
+        total = z_out[n, z].astype(F32)
         for d in range(7):
-            total += z_in[sn, d].astype(F32)
+            total += z_in[n, d].astype(F32)
         return total
 
-    total = z_total(0)
-    for block in range(6):
-        col1[block] = total[block] * (-listed(st1, block * 16 + row))
+    for half in range(2):
+        total = z_total(half, 7 + 8 * half, 0)
+        for step in range(3):
+            block = 3 * half + step
+            col1[block] = total[step] * (-listed(st1, block * 16 + row))
     carry[...] = fdot(col1[...].reshape(48, 256), wide[...])
 
     for g in range(2):
@@ -251,9 +279,14 @@
         for d in (4, 3, 5, 2, 6, 1, 7):
             remote(g_y, g_yin.at[d - 1], 10, g, 2 * lax.rem(y + d, NY) + core, col)
 
-    total = z_total(1).reshape(48, 256) + carry[...]
+    early = z_total(2, 7, 1)
+    wait_bytes(q_xin, recv_sem.at[13, 0])
+    late = q_x[x].astype(F32)
+    for d in range(3):
+        late += q_xin[d].astype(F32)
     for block in range(6):
-        col2[block] = total[8 * block:8 * block + 8, :] * (-listed(st2, block * 16 + row))
+        total = (early if block < 3 else late)[block % 3] + carry[8 * block:8 * block + 8, :]
+        col2[block] = total * (-listed(st2, block * 16 + row))
 
     for g in range(2):
         g_y, g_yin, g_sum = groups[g][6:9]
@@ -281,12 +314,15 @@
             stage_a(zhi, k, r_t, c_t).wait_send()
 
     wait_bytes(rows_z.at[pl.ds(0, 7)], send_sem.at[5, 0])
+    wait_bytes(rows_x.at[pl.ds(0, 3)], send_sem.at[14, 0])
+    wait_bytes(q_in, send_sem.at[12, 0])
+    wait_bytes(q_xin, send_sem.at[13, 0])
     for sn in range(2):
         wait_bytes(raw.at[sn, :, pl.ds(0, 3), core], send_sem.at[1, sn])
         wait_bytes(raw.at[sn, :, :, core], send_sem.at[2, sn])
-        for half in range(2):
-            wait_bytes(part_in.at[sn, half], send_sem.at[3 + half, sn])
-        wait_bytes(z_in.at[sn], send_sem.at[7, sn])
+        for half in range(2 - sn):
+            wait_bytes(part_in.at[2 * sn + half], send_sem.at[3 + half, sn])
+            wait_bytes(z_in.at[2 * sn + half], send_sem.at[7 + 8 * half, sn])
         wait_bytes(groups[sn][1], send_sem.at[6, sn])
         wait_bytes(groups[sn][3], send_sem.at[8, sn])
         wait_bytes(groups[sn][5], send_sem.at[9, sn])
@@ -321,24 +357,30 @@
             pltpu.VMEM((256, 256), F32),
             pltpu.VMEM((256, 256), F32),
             pltpu.VMEM((256, 256), F32),
+            pltpu.VMEM((2, 3, 2, 8, 256), BF16),
             pltpu.VMEM((8, 2, 3, 2, 8, 256), BF16),
-            pltpu.VMEM((8, 6, 8, 256), F32),
+            pltpu.VMEM((4, 3, 2, 8, 256), BF16),
+            pltpu.VMEM((2, 8, 3, 8, 256), F32),
             pltpu.VMEM((2, 256, 384), BF16),
             pltpu.VMEM((2, 3, 4, 2, 4, 8, 256), BF16),
             pltpu.VMEM((2, 3, 256, 256), BF16),
-            pltpu.VMEM((2, 2, 4, 8, 3, 8, 256), BF16),
-            pltpu.VMEM((2, 2, 3, 8, 3, 8, 256), BF16),
-            pltpu.VMEM((8, 6, 8, 256), F32),
-            pltpu.VMEM((2, 8, 6, 8, 256), BF16),
-            pltpu.VMEM((2, 7, 6, 8, 256), BF16),
+            pltpu.VMEM((8, 4, 3, 8, 256), BF16),
+            pltpu.VMEM((7, 4, 3, 8, 256), BF16),
+            pltpu.VMEM((4, 3, 8, 256), BF16),
+            pltpu.VMEM((3, 3, 8, 256), BF16),
+            pltpu.VMEM((3, 4, 8, 3, 8, 256), BF16),
+            pltpu.VMEM((3, 3, 8, 3, 8, 256), BF16),
+            pltpu.VMEM((2, 8, 3, 8, 256), F32),
+            pltpu.VMEM((3, 8, 3, 8, 256), BF16),
+            pltpu.VMEM((3, 7, 3, 8, 256), BF16),
             *e_scratch(2),
             *e_scratch(1),
             pltpu.VMEM((256, 256), F32),
             pltpu.VMEM((48, 256), F32),
             pltpu.SemaphoreType.DMA((8,)),
             pltpu.SemaphoreType.DMA((4,)),
-            pltpu.SemaphoreType.DMA((12, 2)),
-            pltpu.SemaphoreType.DMA((12, 2)),
+            pltpu.SemaphoreType.DMA((16, 2)),
+            pltpu.SemaphoreType.DMA((16, 2)),
         ],
         compiler_params=pltpu.CompilerParams(
             collective_id=0, has_side_effects=True, vmem_limit_bytes=40 * 1024 * 1024),

time: 71.2 us -> 66.8 us (0.938)
  Pallas kernels: 69.2 us -> 64.8 us
    pallas_call x1, Pallas kernels: 69.2 us -> 64.8 us  [body(): pl.pallas_call(kernel, out_shape=jax.ShapeDtypeStruct((15, 8, 256), F32),...]
where the time goes in v3:
time: 66.8 us; the launch traced here: 66.7 us
  Pallas kernels  64.8 us (97%)
  local copies, waits for them, and re-layouts  1.25 us (2%)
    pallas_call x1, Pallas kernels, body(): pl.pallas_call(kernel, out_shape=jax.ShapeDtypeStruct((15, 8, 256), F32),...  64.8 us

profile of v3, /device:TPU:1, one launch (start us, length us, event | category | flops | bytes accessed | tf_op | source)
XLA Modules:
  0.0 66.7 jit_solution(3191474876405809064)
XLA Ops:
  0.6 64.8 %shard_map.119 = f32[15,8,256]{2,1,0:T(8,128)S(1)} custom-call(bf16[6,3,256,256]{3,2,1,0:T(8,128)(2,1)} %bitcast.19, bf16[3,2,8,256]{3,2,1,0:T(8,128)(2,1)} %bitcast.20, bf16[3,2,8,256]{3,2,1,0:T(8,128)(2,1)} %bitcast.21, bf16[256,256]{1,0:T(8,128)(2,1)} %link_hbm.1, f32[256,256]{1,0:T(8,128)} %inv1_hbm.1, f32[256,256]{1,0:T(8,128)} %inv2_hbm.1, ...), custom_call_target="tpu_custom_call" | custom-call | tf_op jit(solution)/shard_map/pallas_call | solution.py:345
  65.4 0.6 slice_bitcast_fusion.2
  66.0 0.6 slice_bitcast_fusion

commit v4 on v3

--- a/solution.py
+++ b/solution.py
@@ -45,7 +45,7 @@
     diag1, link, diag2 = out.at[12], out.at[13], out.at[14]
     y, core = lax.div(row, 2), lax.rem(row, 2)
     z, x = lax.div(col, NX), lax.rem(col, NX)
-    quad = lax.rem(y, 4)
+    part = lax.rem(lax.rem(z, 4) + 2 + lax.div(lax.rem(col, 16), 2) + 4 - lax.rem(y, 4), 4)
 
     loads = [
         pltpu.make_async_copy(p1_hbm, p_v.at[0], load_sem.at[0]),
@@ -67,7 +67,7 @@
 
     src_row = lax.rem(col, 16)
     for slot in range(4):
-        src_col = 4 * (2 * quad + core) + slot
+        src_col = 4 * (4 * core + part) + slot
         me = jnp.logical_and(src_row == row, src_col == col)
 
         @pl.when(jnp.logical_not(me))
@@ -87,7 +87,7 @@
     others = 3 + 7 + 7 + 1
     for zhi in range(2):
         for k in range(2):
-            r_t = 2 * (lax.div(z, 2) + 4 * k) + lax.rem(z, 2)
+            r_t = 2 * (lax.rem(y + 10 - z + lax.div(row, 4), 4) + 4 * k) + lax.div(z, 4)
             c_t = row + 16 * zhi
             me = jnp.logical_and(r_t == row, c_t == col)
             others = others + jnp.where(me, 0, 1)
@@ -107,7 +107,7 @@
     rows_x[x] = rows_z[z, 1]
     pl.semaphore_wait(barrier, others)
 
-    spot_a = raw.at[:, :, lax.div(col, 8), lax.rem(lax.div(col, 4), 2), lax.rem(col, 4)]
+    spot_a = raw.at[:, :, lax.div(z, 4), lax.rem(z, 4), x]
 
     def stage_a(zhi, k, r_t, c_t):
         return pltpu.make_async_remote_copy(
@@ -128,9 +128,9 @@
             src, dst, send_sem.at[stage, sn], recv_sem.at[stage, sn],
             device_id=dev(r, c), device_id_type=pl.DeviceIdType.MESH).start()
 
-    wait_bytes(raw.at[:, :, quad, core], recv_sem.at[0, 0])
-    for sn in range(2):
-        spot = raw.at[sn, :, quad, core]
+    wait_bytes(raw.at[:, :, core, part], recv_sem.at[0, 0])
+    for sn in range(2):
+        spot = raw.at[sn, :, core, part]
         for d in (2 + 4 * sn, 1, 7):
             remote(spot, spot, 1, sn, 2 * lax.rem(y + d, NY) + core, col)
     for d in (4, 3, 5, 2, 6, 1, 7):
@@ -139,13 +139,13 @@
         remote(rows_x.at[x], rows_x.at[x], 14, 0, row, 4 * z + lax.rem(x + d, NX))
     wide[...] = fdot(link_v[...].astype(F32), inv_v[1])
     for sn in range(2):
-        wait_bytes(raw.at[sn, :, pl.ds(0, 3), core], recv_sem.at[1, sn])
-        spot = raw.at[sn, :, :, core]
+        wait_bytes(raw.at[sn, :, core, pl.ds(0, 3)], recv_sem.at[1, sn])
+        spot = raw.at[sn, :, core]
         remote(spot, spot, 2, sn, twin, col)
     loads[-1].wait()
 
     for sn in range(2):
-        wait_bytes(raw.at[sn, :, :, core], recv_sem.at[2, sn])
+        wait_bytes(raw.at[sn, :, core], recv_sem.at[2, sn])
         for b in range(3):
             fac[sn, b] = raw[sn, b].astype(F32).reshape(256, 256).astype(BF16)
         for half in ((0, 1) if sn == 0 else (1, 0)):
@@ -192,6 +192,33 @@
 
     groups = ((ea_own, ea_twin, ea_out, ea_in, ea_z, ea_zin, ea_y, ea_yin, ea_sum),
               (eb_own, eb_twin, eb_out, eb_in, eb_z, eb_zin, eb_y, eb_yin, eb_sum))
+
+    def send_z(n, half, sn):
+        for d in (4, 3, 5, 2, 6, 1, 7):
+            to = lax.rem(z + d, NZ)
+            remote(z_out.at[n, to], z_in.at[n, d - 1], 7 + 8 * half, sn, row, 4 * to + x)
+
+    def sum_x(g):
+        g_out, g_in, g_z, g_zin = groups[g][2:6]
+        wait_bytes(g_in, recv_sem.at[8, g])
+        total = g_out[x].astype(F32)
+        for d in range(3):
+            total += g_in[d].astype(F32)
+        g_z[...] = total.astype(BF16)
+        for d in (4, 3, 5, 2, 6, 1, 7):
+            to = lax.rem(z + d, NZ)
+            remote(g_z.at[to], g_zin.at[d - 1], 9, g, row, 4 * to + x)
+
+    def sum_z(g):
+        g_z, g_zin, g_y, g_yin = groups[g][4:8]
+        wait_bytes(g_zin, recv_sem.at[9, g])
+        total = g_z[z].astype(F32)
+        for d in range(7):
+            total += g_zin[d].astype(F32)
+        g_y[...] = total
+        for d in (4, 3, 5, 2, 6, 1, 7):
+            remote(g_y, g_yin.at[d - 1], 10, g, 2 * lax.rem(y + d, NY) + core, col)
+
     for sn in range(2):
         for half in range(2 - sn):
             n = 2 * sn + half
@@ -201,9 +228,8 @@
                 total += part_in[n, d].astype(F32)
             summed[half] = total
             z_out[n] = total.astype(BF16)
-            for d in (4, 3, 5, 2, 6, 1, 7):
-                to = lax.rem(z + d, NZ)
-                remote(z_out.at[n, to], z_in.at[n, d - 1], 7 + 8 * half, sn, row, 4 * to + x)
+            if sn == 0:
+                send_z(n, half, sn)
         depth = 384 - 192 * sn
         sums = (summed[...] if sn == 0 else summed[0]).reshape(depth, 256)
         high = sums.astype(BF16)
@@ -228,12 +254,14 @@
             for d in range(7):
                 total += q_in[d].astype(F32)
             q_x[...] = total.astype(BF16)
+            late = jnp.stack([rows_x[:, block // 2, block % 2].astype(F32) for block in (3, 4, 5)], axis=1)
+            spread_rows(g_own, 0, second - tdot(late.reshape(96, 256), total.reshape(96, 256)))
+        remote(g_own.at[1 - core], g_twin, 6, sn, twin, col)
+        if sn:
+            send_z(2, 0, 1)
             for d in (2, 1, 3):
                 to = lax.rem(x + d, NX)
                 remote(q_x.at[to], q_xin.at[d - 1], 13, 0, row, 4 * z + to)
-            late = jnp.stack([rows_x[:, block // 2, block % 2].astype(F32) for block in (3, 4, 5)], axis=1)
-            spread_rows(g_own, 0, second - tdot(late.reshape(96, 256), total.reshape(96, 256)))
-        remote(g_own.at[1 - core], g_twin, 6, sn, twin, col)
         if sn == 0:
             rest[...] = fdot(tall[...], fdot(first, wide[...]) - top) - fdot(top_t, wide[...])
         wait_bytes(g_twin, recv_sem.at[6, sn])
@@ -242,18 +270,11 @@
             to = lax.rem(x + d, NX)
             remote(g_out.at[to], g_in.at[d - 1], 8, sn, row, 4 * z + to)
 
-    for g in range(2):
-        g_out, g_in, g_z, g_zin = groups[g][2:6]
-        wait_bytes(g_in, recv_sem.at[8, g])
-        total = g_out[x].astype(F32)
-        for d in range(3):
-            total += g_in[d].astype(F32)
-        g_z[...] = total.astype(BF16)
-        for d in (4, 3, 5, 2, 6, 1, 7):
-            to = lax.rem(z + d, NZ)
-            remote(g_z.at[to], g_zin.at[d - 1], 9, g, row, 4 * to + x)
+    sum_x(0)
     gram1[...] = tdot(inv_v[0], inv_v[0])
     gram2[...] = tdot(inv_v[1], inv_v[1]) + fdot(tall[...], fdot(gram1[...], wide[...]))
+    sum_x(1)
+    sum_z(0)
 
     def z_total(n, stage, sn):
         wait_bytes(z_in.at[n], recv_sem.at[stage, sn])
@@ -268,16 +289,7 @@
             block = 3 * half + step
             col1[block] = total[step] * (-listed(st1, block * 16 + row))
     carry[...] = fdot(col1[...].reshape(48, 256), wide[...])
-
-    for g in range(2):
-        g_z, g_zin, g_y, g_yin = groups[g][4:8]
-        wait_bytes(g_zin, recv_sem.at[9, g])
-        total = g_z[z].astype(F32)
-        for d in range(7):
-            total += g_zin[d].astype(F32)
-        g_y[...] = total
-        for d in (4, 3, 5, 2, 6, 1, 7):
-            remote(g_y, g_yin.at[d - 1], 10, g, 2 * lax.rem(y + d, NY) + core, col)
+    sum_z(1)
 
     early = z_total(2, 7, 1)
     wait_bytes(q_xin, recv_sem.at[13, 0])
@@ -288,7 +300,13 @@
         total = (early if block < 3 else late)[block % 3] + carry[8 * block:8 * block + 8, :]
         col2[block] = total * (-listed(st2, block * 16 + row))
 
-    for g in range(2):
+    at = pl.multiple_of(8 * col, 8)
+
+    def whole(g, m):
+        g_sum = groups[g][8]
+        return jnp.concatenate([g_sum[0, m], g_sum[1, m]], axis=1)
+
+    def sum_y(g):
         g_y, g_yin, g_sum = groups[g][6:9]
         wait_bytes(g_yin, recv_sem.at[10, g])
         total = g_y[...]
@@ -296,17 +314,14 @@
             total += g_yin[d]
         g_sum[core] = total
         remote(g_sum.at[core], g_sum.at[core], 11, g, twin, col)
-    for g in range(2):
-        wait_bytes(groups[g][8].at[core], recv_sem.at[11, g])
-
-    at = pl.multiple_of(8 * col, 8)
-
-    def whole(g_sum, m):
-        return jnp.concatenate([g_sum[0, m], g_sum[1, m]], axis=1)
-
-    diag1[...] = gram1[pl.ds(at, 8), :] - whole(ea_sum, 0)
-    link[...] = -(whole(ea_sum, 1) + fdot(diag1[...], wide[...]))
-    diag2[...] = gram2[pl.ds(at, 8), :] - whole(eb_sum, 0)
+
+    sum_y(0)
+    wait_bytes(ea_sum.at[core], recv_sem.at[11, 0])
+    diag1[...] = gram1[pl.ds(at, 8), :] - whole(0, 0)
+    link[...] = -(whole(0, 1) + fdot(diag1[...], wide[...]))
+    sum_y(1)
+    wait_bytes(eb_sum.at[core], recv_sem.at[11, 1])
+    diag2[...] = gram2[pl.ds(at, 8), :] - whole(1, 0)
 
     for zhi, k, r_t, c_t, me in targets:
         @pl.when(jnp.logical_not(me))
@@ -318,8 +333,8 @@
     wait_bytes(q_in, send_sem.at[12, 0])
     wait_bytes(q_xin, send_sem.at[13, 0])
     for sn in range(2):
-        wait_bytes(raw.at[sn, :, pl.ds(0, 3), core], send_sem.at[1, sn])
-        wait_bytes(raw.at[sn, :, :, core], send_sem.at[2, sn])
+        wait_bytes(raw.at[sn, :, core, pl.ds(0, 3)], send_sem.at[1, sn])
+        wait_bytes(raw.at[sn, :, core], send_sem.at[2, sn])
         for half in range(2 - sn):
             wait_bytes(part_in.at[2 * sn + half], send_sem.at[3 + half, sn])
             wait_bytes(z_in.at[2 * sn + half], send_sem.at[7 + 8 * half, sn])
@@ -362,7 +377,7 @@
             pltpu.VMEM((4, 3, 2, 8, 256), BF16),
             pltpu.VMEM((2, 8, 3, 8, 256), F32),
             pltpu.VMEM((2, 256, 384), BF16),
-            pltpu.VMEM((2, 3, 4, 2, 4, 8, 256), BF16),
+            pltpu.VMEM((2, 3, 2, 4, 4, 8, 256), BF16),
             pltpu.VMEM((2, 3, 256, 256), BF16),
             pltpu.VMEM((8, 4, 3, 8, 256), BF16),
             pltpu.VMEM((7, 4, 3, 8, 256), BF16),
@@ -378,7 +393,7 @@
             pltpu.VMEM((256, 256), F32),
             pltpu.VMEM((48, 256), F32),
             pltpu.SemaphoreType.DMA((8,)),
-            pltpu.SemaphoreType.DMA((4,)),
+            pltpu.SemaphoreType.DMA((8,)),
             pltpu.SemaphoreType.DMA((16, 2)),
             pltpu.SemaphoreType.DMA((16, 2)),
         ],

time: 66.8 us -> 65.1 us (0.975)
  Pallas kernels: 64.8 us -> 63 us
    pallas_call x1, Pallas kernels: 64.8 us -> 63 us  [body(): pl.pallas_call(kernel, out_shape=jax.ShapeDtypeStruct((15, 8, 256), F32),...]
where the time goes in v4:
time: 65.1 us; the launch traced here: 64.9 us
  Pallas kernels  63 us (97%)
  local copies, waits for them, and re-layouts  1.25 us (2%)
    pallas_call x1, Pallas kernels, body(): pl.pallas_call(kernel, out_shape=jax.ShapeDtypeStruct((15, 8, 256), F32),...  63 us

profile of v4, /device:TPU:1, one launch (start us, length us, event | category | flops | bytes accessed | tf_op | source)
XLA Modules:
  0.0 64.9 jit_solution(13189503797905084965)
XLA Ops:
  0.6 63.0 %shard_map.119 = f32[15,8,256]{2,1,0:T(8,128)S(1)} custom-call(bf16[6,3,256,256]{3,2,1,0:T(8,128)(2,1)} %bitcast.19, bf16[3,2,8,256]{3,2,1,0:T(8,128)(2,1)} %bitcast.20, bf16[3,2,8,256]{3,2,1,0:T(8,128)(2,1)} %bitcast.21, bf16[256,256]{1,0:T(8,128)(2,1)} %link_hbm.1, f32[256,256]{1,0:T(8,128)} %inv1_hbm.1, f32[256,256]{1,0:T(8,128)} %inv2_hbm.1, ...), custom_call_target="tpu_custom_call" | custom-call | tf_op jit(solution)/shard_map/pallas_call | solution.py:360
  63.7 0.6 slice_bitcast_fusion.2
  64.3 0.6 slice_bitcast_fusion

commit v5 on v4

--- a/solution.py
+++ b/solution.py
@@ -34,7 +34,7 @@
 def kernel(
     s_hbm, p1_hbm, p2_hbm, link_hbm, inv1_hbm, inv2_hbm, st1_hbm, st2_hbm,
     out,
-    st1, st2, s_v, link_v, inv_v, wide, tall, gram1, gram2, p_v, rows_z, rows_x, ordered, fac_t, raw, fac,
+    st1, st2, s_v, link_v, inv_v, wide, tall, gram1, gram2, p_v, rows_z, rows_x, ordered, fac_t, late_t, raw, fac,
     q_out, q_in, q_x, q_xin, part_out, part_in, summed, z_out, z_in,
     ea_own, ea_twin, ea_out, ea_in, ea_z, ea_zin, ea_y, ea_yin, ea_sum,
     eb_own, eb_twin, eb_out, eb_in, eb_z, eb_zin, eb_y, eb_yin, eb_sum, rest, carry,
@@ -181,7 +181,12 @@
         for block in range(6):
             ordered[block // 3, :, block % 3] = rows_z[:, sn, block // 2, block % 2].astype(F32)
         fac_t[sn] = ordered[...].reshape(384, 256).T.astype(BF16)
+    blank = jnp.zeros((32, 256), F32)
+    late = jnp.stack([rows_x[:, block // 2, block % 2].astype(F32) for block in (3, 4, 5)], axis=1)
+    late_t[...] = jnp.concatenate([late.reshape(96, 256), blank], axis=0).T.astype(BF16)
     tall[...] = wide[...].T
+    gram1[...] = tdot(inv_v[0], inv_v[0])
+    gram2[...] = tdot(inv_v[1], inv_v[1]) + fdot(tall[...], fdot(gram1[...], wide[...]))
 
     def spread_rows(to, m, matrix):
         for xd in range(NX):
@@ -254,8 +259,12 @@
             for d in range(7):
                 total += q_in[d].astype(F32)
             q_x[...] = total.astype(BF16)
-            late = jnp.stack([rows_x[:, block // 2, block % 2].astype(F32) for block in (3, 4, 5)], axis=1)
-            spread_rows(g_own, 0, second - tdot(late.reshape(96, 256), total.reshape(96, 256)))
+            sums = jnp.concatenate([total.reshape(96, 256), blank], axis=0)
+            high = sums.astype(BF16)
+            low = (sums - high.astype(F32)).astype(BF16)
+            second -= (jnp.dot(late_t[...], high, preferred_element_type=F32)
+                       + jnp.dot(late_t[...], low, preferred_element_type=F32))
+            spread_rows(g_own, 0, second)
         remote(g_own.at[1 - core], g_twin, 6, sn, twin, col)
         if sn:
             send_z(2, 0, 1)
@@ -271,8 +280,6 @@
             remote(g_out.at[to], g_in.at[d - 1], 8, sn, row, 4 * z + to)
 
     sum_x(0)
-    gram1[...] = tdot(inv_v[0], inv_v[0])
-    gram2[...] = tdot(inv_v[1], inv_v[1]) + fdot(tall[...], fdot(gram1[...], wide[...]))
     sum_x(1)
     sum_z(0)
 
@@ -315,14 +322,6 @@
         g_sum[core] = total
         remote(g_sum.at[core], g_sum.at[core], 11, g, twin, col)
 
-    sum_y(0)
-    wait_bytes(ea_sum.at[core], recv_sem.at[11, 0])
-    diag1[...] = gram1[pl.ds(at, 8), :] - whole(0, 0)
-    link[...] = -(whole(0, 1) + fdot(diag1[...], wide[...]))
-    sum_y(1)
-    wait_bytes(eb_sum.at[core], recv_sem.at[11, 1])
-    diag2[...] = gram2[pl.ds(at, 8), :] - whole(1, 0)
-
     for zhi, k, r_t, c_t, me in targets:
         @pl.when(jnp.logical_not(me))
         def _():
@@ -341,6 +340,16 @@
         wait_bytes(groups[sn][1], send_sem.at[6, sn])
         wait_bytes(groups[sn][3], send_sem.at[8, sn])
         wait_bytes(groups[sn][5], send_sem.at[9, sn])
+
+    sum_y(0)
+    wait_bytes(ea_sum.at[core], recv_sem.at[11, 0])
+    diag1[...] = gram1[pl.ds(at, 8), :] - whole(0, 0)
+    link[...] = -(whole(0, 1) + fdot(diag1[...], wide[...]))
+    sum_y(1)
+    wait_bytes(eb_sum.at[core], recv_sem.at[11, 1])
+    diag2[...] = gram2[pl.ds(at, 8), :] - whole(1, 0)
+
+    for sn in range(2):
         wait_bytes(groups[sn][7], send_sem.at[10, sn])
         wait_bytes(groups[sn][8].at[core], send_sem.at[11, sn])
 
@@ -377,6 +386,7 @@
             pltpu.VMEM((4, 3, 2, 8, 256), BF16),
             pltpu.VMEM((2, 8, 3, 8, 256), F32),
             pltpu.VMEM((2, 256, 384), BF16),
+            pltpu.VMEM((256, 128), BF16),
             pltpu.VMEM((2, 3, 2, 4, 4, 8, 256), BF16),
             pltpu.VMEM((2, 3, 256, 256), BF16),
             pltpu.VMEM((8, 4, 3, 8, 256), BF16),

time: 65.1 us -> 64.8 us (level)
  no operation moved by 1% of the time
where the time goes in v5:
time: 64.8 us; the launch traced here: 64.6 us
  Pallas kernels  62.7 us (97%)
  local copies, waits for them, and re-layouts  1.25 us (2%)
    pallas_call x1, Pallas kernels, body(): pl.pallas_call(kernel, out_shape=jax.ShapeDtypeStruct((15, 8, 256), F32),...  62.7 us

profile of v5, /device:TPU:1, one launch (start us, length us, event | category | flops | bytes accessed | tf_op | source)
XLA Modules:
  0.0 64.6 jit_solution(11612570260288470837)
XLA Ops:
  0.6 62.7 %shard_map.119 = f32[15,8,256]{2,1,0:T(8,128)S(1)} custom-call(bf16[6,3,256,256]{3,2,1,0:T(8,128)(2,1)} %bitcast.19, bf16[3,2,8,256]{3,2,1,0:T(8,128)(2,1)} %bitcast.20, bf16[3,2,8,256]{3,2,1,0:T(8,128)(2,1)} %bitcast.21, bf16[256,256]{1,0:T(8,128)(2,1)} %link_hbm.1, f32[256,256]{1,0:T(8,128)} %inv1_hbm.1, f32[256,256]{1,0:T(8,128)} %inv2_hbm.1, ...), custom_call_target="tpu_custom_call" | custom-call | tf_op jit(solution)/shard_map/pallas_call | solution.py:369
  63.4 0.6 slice_bitcast_fusion.2
  64.0 0.6 slice_bitcast_fusion

commit v6 on v5

--- a/solution.py
+++ b/solution.py
@@ -131,7 +131,10 @@
     wait_bytes(raw.at[:, :, core, part], recv_sem.at[0, 0])
     for sn in range(2):
         spot = raw.at[sn, :, core, part]
-        for d in (2 + 4 * sn, 1, 7):
+        for d, at in ((2, 0), (6, 2)):
+            near = raw.at[sn, :, core, part, pl.ds(at, 2)]
+            remote(near, near, 1, sn, 2 * lax.rem(y + d, NY) + core, col)
+        for d in (1, 7):
             remote(spot, spot, 1, sn, 2 * lax.rem(y + d, NY) + core, col)
     for d in (4, 3, 5, 2, 6, 1, 7):
         remote(rows_z.at[z], rows_z.at[z], 5, 0, row, 4 * lax.rem(z + d, NZ) + x)

time: 64.8 us -> 65 us (level)
  no operation moved by 1% of the time
where the time goes in v6:
time: 65 us; the launch traced here: 64.8 us
  Pallas kernels  62.9 us (97%)
  local copies, waits for them, and re-layouts  1.25 us (2%)
    pallas_call x1, Pallas kernels, body(): pl.pallas_call(kernel, out_shape=jax.ShapeDtypeStruct((15, 8, 256), F32),...  62.9 us

profile of v6, /device:TPU:1, one launch (start us, length us, event | category | flops | bytes accessed | tf_op | source)
XLA Modules:
  0.0 64.8 jit_solution(6164513308131810338)
XLA Ops:
  0.6 62.9 %shard_map.119 = f32[15,8,256]{2,1,0:T(8,128)S(1)} custom-call(bf16[6,3,256,256]{3,2,1,0:T(8,128)(2,1)} %bitcast.19, bf16[3,2,8,256]{3,2,1,0:T(8,128)(2,1)} %bitcast.20, bf16[3,2,8,256]{3,2,1,0:T(8,128)(2,1)} %bitcast.21, bf16[256,256]{1,0:T(8,128)(2,1)} %link_hbm.1, f32[256,256]{1,0:T(8,128)} %inv1_hbm.1, f32[256,256]{1,0:T(8,128)} %inv2_hbm.1, ...), custom_call_target="tpu_custom_call" | custom-call | tf_op jit(solution)/shard_map/pallas_call | solution.py:372
  63.6 0.6 slice_bitcast_fusion.2
  64.2 0.6 slice_bitcast_fusion
